TPU v7x, 768 devices: a whole 4x8x12 slice. The times are simulated.
768 devices in a mesh: fsdp: 24 (over z, x_lo), expert: 32 (over x_hi, y, core).
Axes of the slice: x: 4 (x_hi: 2, x_lo: 2; x = x_hi * 2 + x_lo), y: 8, z: 12, core: 2. Of those that a mesh axis runs over, the one named last changes fastest.
Arguments:
- tokens: bfloat16 [2048, 6144], P('expert', 'fsdp'), may hold values from -6 to 6
- expert_ids: int32 [2048, 2], P('expert'), may hold values from 0 to 7, all different within a row; in each aligned block of 64 rows (0 to 63, 64 to 127, ...) at most 24 rows name the same one
- gate_values: float32 [2048, 2], P('expert'), may hold values from 0.1 to 1
- w_gate: bfloat16 [6144, 65536], P('fsdp', 'expert'), may hold values from -0.078125 to 0.078125
- w_up: bfloat16 [6144, 65536], P('fsdp', 'expert'), may hold values from -0.078125 to 0.078125
- w_down: bfloat16 [65536, 6144], P('expert', 'fsdp'), may hold values from -0.0625 to 0.0625
- scale_gate: float32 [48, 512], P('fsdp', 'expert'), may hold values from 0.5 to 2
- scale_up: float32 [48, 512], P('fsdp', 'expert'), may hold values from 0.5 to 2
- scale_down: float32 [512, 48], P('expert', 'fsdp'), may hold values from 0.5 to 2
Outputs:
- mixed: bfloat16 [2048, 6144], P('expert', 'fsdp')
Inputs may be any that keep to these rules, and one draw needn't show every extreme that they name: `expert_ids`: within the 64 rows of each index of expert (aligned blocks of rows), no expert id occurs in more than 24 rows, and some id occurs in exactly 24 rows of some block; the two ids of a row differ; every id occurs somewhere.
All inputs are finite; a program needn't handle non-finite values.
Results may differ from a plain program's by a relative error of at most 0.03.
Values may be sent and summed in bfloat16 or wider, within the bound.
A program may use at most 32 MiB of HBM per device.

v0:
```python
import jax
import jax.numpy as jnp
from jax import lax
from jax.sharding import PartitionSpec as P

EXPERTS = 8
BLOCK = 128
CAP = 24


def rounded(values):
    return lax.optimization_barrier(values.astype(jnp.bfloat16)).astype(jnp.float32)


def dequant(weights, block_scale):
    spread = jnp.repeat(jnp.repeat(block_scale, BLOCK, axis=0), BLOCK, axis=1)
    return (weights.astype(jnp.float32) * spread).astype(jnp.bfloat16)


def shards(tokens, expert_ids, gate_values, w_gate, w_up, w_down, scale_gate, scale_up, scale_down):
    device_count = lax.axis_size("expert")
    slices = device_count // EXPERTS
    local_tokens = tokens.shape[0]
    feature_cols = tokens.shape[1]
    slot_total = EXPERTS * CAP
    flat_ids = expert_ids.reshape(-1)
    onehot = (flat_ids[:, None] == jnp.arange(EXPERTS, dtype=jnp.int32)[None, :]).astype(jnp.int32)
    slot_rank = jnp.sum((jnp.cumsum(onehot, axis=0) - onehot) * onehot, axis=1)
    target = flat_ids * CAP + slot_rank
    placing = (target[:, None] == jnp.arange(slot_total, dtype=jnp.int32)[None, :]).astype(
        jnp.float32
    )
    token_map = jnp.sum(placing.reshape(local_tokens, 2, slot_total), axis=1).astype(jnp.bfloat16)
    packed = jnp.einsum("ts,td->sd", token_map, tokens, preferred_element_type=jnp.float32).astype(
        jnp.bfloat16
    )
    outgoing = jnp.broadcast_to(
        packed.reshape(EXPERTS, 1, CAP, feature_cols), (EXPERTS, slices, CAP, feature_cols)
    ).reshape(device_count * CAP, feature_cols)
    incoming = lax.all_to_all(outgoing, "expert", split_axis=0, concat_axis=0, tiled=True)
    down_deq = dequant(w_down, scale_down)

    def make_term(weights):
        return rounded(jnp.dot(incoming, weights, preferred_element_type=jnp.float32))

    gate_sum = lax.psum_scatter(
        make_term(dequant(w_gate, scale_gate)).astype(jnp.bfloat16),
        "fsdp",
        scatter_dimension=0,
        tiled=True,
    ).astype(jnp.float32)
    up_sum = lax.psum_scatter(
        make_term(dequant(w_up, scale_up)).astype(jnp.bfloat16),
        "fsdp",
        scatter_dimension=0,
        tiled=True,
    ).astype(jnp.float32)
    hidden = (jax.nn.silu(gate_sum) * up_sum).astype(jnp.bfloat16)
    partial_rows = jnp.dot(
        lax.all_gather(hidden, "fsdp", axis=0, tiled=True),
        down_deq,
        preferred_element_type=jnp.float32,
    ).astype(jnp.bfloat16)
    returned = lax.all_to_all(partial_rows, "expert", split_axis=0, concat_axis=0, tiled=True)
    slice_sums = jnp.sum(
        returned.reshape(EXPERTS, slices, CAP, feature_cols).astype(jnp.float32), axis=1
    )
    slice_sums = slice_sums.reshape(slot_total, feature_cols)
    weights_map = jnp.sum(
        (placing * gate_values.reshape(-1)[:, None]).reshape(local_tokens, 2, slot_total), axis=1
    )
    mixed_rows = jnp.dot(
        weights_map, slice_sums, precision=lax.Precision.HIGHEST, preferred_element_type=jnp.float32
    )
    return mixed_rows.astype(jnp.bfloat16)


def solution(mesh):
    in_specs = (
        P("expert", "fsdp"),
        P("expert", None),
        P("expert", None),
        P("fsdp", "expert"),
        P("fsdp", "expert"),
        P("expert", "fsdp"),
        P("fsdp", "expert"),
        P("fsdp", "expert"),
        P("expert", "fsdp"),
    )
    out_specs = P("expert", "fsdp")
    return jax.shard_map(shards, mesh=mesh, in_specs=in_specs, out_specs=out_specs, check_vma=False)
```

profile of v0, /device:TPU:1, one launch (start us, length us, event | category | flops | bytes accessed | tf_op | source)
XLA Modules:
  0.0 420.3 jit_solution(5018974145876577403)
XLA Ops:
  6.5 0.8 copy.25
  7.3 0.1 eq.30
  7.5 0.1 fusion.11
  7.6 0.2 reduce_window_sum.11
  7.7 0.2 select_reduce_fusion.1
  7.9 0.1 reduce_sum.39
  8.1 0.1 copy.26
  8.1 0.7 multiply_add_fusion
  8.8 0.8 convert_reduce_fusion.1
  9.6 0.2 convolution_convert_fusion.3
  9.9 28.8 %all_to_all.21 = bf16[32,24,256]{2,1,0:T(8,128)(2,1)S(1)} all-to-all(bf16[32,24,256]{2,1,0:T(8,128)(2,1)S(1)} %bitcast.43), channel_id=1, replica_groups=mesh['fsdp'=24,'expert'=32] {'expert'}, dimensions={0} | all-to-all | bytes 786432 | tf_op jit(solution)/shard_map/all_to_all | solution.py:40
  38.7 0.7 broadcast_in_dim.32
  39.4 0.6 broadcast_in_dim.33
  40.0 2.8 convolution_convert_fusion
  42.8 0.0 reduce-scatter.5.cloned.1.call-update
  42.9 0.0 reduce-scatter.3.cloned.1.call-start
  42.9 0.6 copy-done.5
  43.5 0.6 broadcast_in_dim.31
  44.1 2.9 convolution_convert_fusion.1
  47.0 0.0 reduce-scatter.3.cloned.1.call-update
  47.0 0.0 all-gather.2.cloned.1.call-start
  47.1 92.5 %reduce-scatter.5.cloned.1.call-done = bf16[32,2048]{1,0:T(8,128)(2,1)} async-done(((bf16[768,2048]{1,0:T(8,128)(2,1)}), bf16[32,2048]{1,0:T(8,128)(2,1)}) %reduce-scatter.5.cloned.1.call-update) | async-done | bytes 131088 | tf_op jit(solution)/shard_map/reduce_scatter | solution.py:52
  139.6 115.4 %reduce-scatter.3.cloned.1.call-done = bf16[32,2048]{1,0:T(8,128)(2,1)} async-done(((bf16[768,2048]{1,0:T(8,128)(2,1)}), bf16[32,2048]{1,0:T(8,128)(2,1)}) %reduce-scatter.3.cloned.1.call-update) | async-done | bytes 131088 | tf_op jit(solution)/shard_map/reduce_scatter | solution.py:46
  255.0 1.7 fusion.10
  256.7 0.0 all-gather.2.cloned.1.call-update
  256.8 0.1 copy.27
  256.9 109.6 %all-gather.2.cloned.1.call-done = bf16[768,2048]{1,0:T(8,128)(2,1)} async-done(((bf16[32,2048]{1,0:T(8,128)(2,1)}), bf16[768,2048]{1,0:T(8,128)(2,1)}) %all-gather.2.cloned.1.call-update) | async-done | bytes 3145744 | tf_op jit(solution)/shard_map/all_gather | solution.py:60
  366.5 0.1 broadcast_in_dim.34
  366.5 4.7 %broadcast_in_dim.35 = f32[2048,2,128]{2,1,0:T(2,128)S(1)} broadcast(f32[2048,2]{1,0:T(8,128)S(1)} %bitcast.41), dimensions={0,1} | broadcast | bytes 2113536 | tf_op jit(solution)/shard_map/broadcast_in_dim | solution.py:16
  371.3 1.0 convolution_convert_fusion.2
  372.3 40.5 %all_to_all.22 = bf16[32,24,256]{2,1,0:T(8,128)(2,1)S(1)} all-to-all(bf16[32,24,256]{2,1,0:T(8,128)(2,1)S(1)} %bitcast.42), channel_id=1, replica_groups=mesh['fsdp'=24,'expert'=32] {'expert'}, dimensions={0} | all-to-all | bytes 786432 | tf_op jit(solution)/shard_map/all_to_all | solution.py:64
  412.9 0.8 convolution_convert_fusion.4
  (17 shorter events, 0.1 us)
Async XLA Ops:
  6.5 3.1 copy-start
  6.5 133.1 %reduce-scatter.5.cloned.1.call-start = ((), (), s32[]{:S(2)}) async-start(), calls=%async_computation.5 | async-start | bytes 3276800 | tf_op jit(solution)/shard_map/reduce_scatter | solution.py:52
  7.6 32.4 %copy-start.2 = (bf16[256,2048]{1,0:T(8,128)(2,1)S(1)}, bf16[256,2048]{1,0:T(8,128)(2,1)}, u32[]{:S(2)}) copy-start(bf16[256,2048]{1,0:T(8,128)(2,1)} %param.13) | copy-start | bytes 3145732
  42.8 0.7 copy-start.5
  42.8 1.3 copy-start.3
  42.9 212.2 %reduce-scatter.3.cloned.1.call-start = ((), (), s32[]{:S(2)}) async-start(), calls=%async_computation.4 | async-start | bytes 3276800 | tf_op jit(solution)/shard_map/reduce_scatter | solution.py:46
  47.0 209.8 %copy-start.6 = (f32[16,2]{0,1:T(2,128)S(1)}, f32[16,2]{0,1:T(2,128)}, u32[]{:S(2)}) copy-start(f32[16,2]{0,1:T(2,128)} %param.17) | copy-start | bytes 388
  47.0 319.4 %all-gather.2.cloned.1.call-start = ((), (), s32[]{:S(2)}) async-start(), calls=%async_computation.6 | async-start | bytes 3276800 | tf_op jit(solution)/shard_map/all_gather | solution.py:60
  256.9 114.4 %copy-start.4 = (bf16[2048,256]{1,0:T(8,128)(2,1)S(1)}, bf16[2048,256]{1,0:T(8,128)(2,1)}, u32[]{:S(2)}) copy-start(bf16[2048,256]{1,0:T(8,128)(2,1)} %param.14) | copy-start | bytes 3145732
  366.5 4.8 %copy-start.1 = (bf16[768,2048]{1,0:T(8,128)(2,1)S(1)}, bf16[768,2048]{1,0:T(8,128)(2,1)}, u32[]{:S(2)}) copy-start(bf16[768,2048]{1,0:T(8,128)(2,1)} %all-gather.2.cloned.1.call-done) | copy-start | bytes 9437188
Sparse Core Ops, SparseCore 0:
  43.0 96.5 reduce-scatter.4
  142.7 112.2 reduce-scatter.2
  257.4 108.9 all-gather.1
where the time goes:
time: 421 us; the launch traced here: 420 us
  waiting for transfers between devices  318 us (76%)
  blocking collectives  69.3 us (16%)
  between operations  13.2 us (3%)
  local copies, waits for them, and re-layouts  8.5 us (2%)
  matrix products  7.79 us (2%)
    reduce_scatter x1, waiting for transfers between devices, shards(): lax.psum_scatter(make_term(dequant(w_gate, scale_gate)).astype(jnp.bfloat...  115 us
    all_gather x1, waiting for transfers between devices, shards(): lax.all_gather(hidden, 'fsdp', axis=0, tiled=True)  110 us
    reduce_scatter x1, waiting for transfers between devices, shards(): lax.psum_scatter(make_term(dequant(w_up, scale_up)).astype(jnp.bfloat16),...  92.5 us
    all_to_all x1, blocking collectives, shards(): lax.all_to_all(partial_rows, 'expert', split_axis=0, concat_axis=0, tiled...  40.5 us
    all_to_all x1, blocking collectives, shards(): lax.all_to_all(outgoing, 'expert', split_axis=0, concat_axis=0, tiled=True)  28.8 us
  transfers between devices with their start and end apart: 3, of which 3 were waited for; matrix products, arithmetic and copies ran while one was open for 1% of the time, Pallas kernels for 0%

commit v1 on v0

v1 whole, which is shorter than its diff:
```python
import functools

import jax
import jax.numpy as jnp
from jax import lax
from jax.experimental import pallas as pl
from jax.experimental.pallas import tpu as pltpu
from jax.sharding import PartitionSpec as P

EXPERTS = 8
BLOCK = 128
CAP = 24
PIECES = 4
OFFSETS = (0, 1, 2, 3)
MESH = pl.DeviceIdType.MESH


def schedule(half):
    tasks = []
    for piece in range(PIECES):
        begin = OFFSETS[piece]
        tasks.append((begin - 0.5, 0, "mul", piece, 0))
        for hop in range(half, 0, -1):
            tasks.append((begin + half - hop, 1, "sum", piece, hop))
        tasks.append((begin + half, 2, "act", piece, 0))
    for part in range(2):
        begin = max(OFFSETS[2 * part], OFFSETS[2 * part + 1]) + half
        for hop in range(1, half + 1):
            tasks.append((begin + hop - 0.5, 3, "gather", part, hop))
    begin = max(OFFSETS) + half
    tasks.append((begin + 0.6, 4, "down", 0, 0))
    for hop in range(1, half + 1):
        tasks.append((begin + hop + 0.6, 4, "down", 0, hop))
    return sorted(tasks)


def expert_kernel(
    ring,
    x_ref,
    wg_ref,
    wu_ref,
    wd_ref,
    sg_ref,
    su_ref,
    sd_ref,
    out_ref,
    x_all,
    w_send,
    w_all,
    d_send,
    d_own,
    d_far,
    parts,
    sum_out,
    sum_in,
    hidden,
    y_own,
    y_out,
    y_in,
    x_sems,
    w_sems,
    sum_sems,
    gather_sems,
    y_sems,
):
    half = ring // 2
    width = x_ref.shape[1]
    rows = x_ref.shape[0]
    chunk = rows // ring
    units = wg_ref.shape[1] // 2
    cols = units // PIECES
    place = lax.axis_index("fsdp")
    z = place // 2
    side = place % 2
    mate = {"fsdp": z * 2 + (1 - side)}
    step = {
        0: {"fsdp": ((z + 1) % ring) * 2 + side},
        1: {"fsdp": ((z + ring - 1) % ring) * 2 + side},
    }
    sends = []

    def remote(src, dst, sems, index, target):
        return pltpu.make_async_remote_copy(
            src_ref=src,
            dst_ref=dst,
            send_sem=sems.at[(0,) + index],
            recv_sem=sems.at[(1,) + index],
            device_id=target,
            device_id_type=MESH,
        )

    def send(*args):
        copy = remote(*args)
        copy.start()
        sends.append(copy)

    barrier = pltpu.get_barrier_semaphore()
    for target in (mate, step[0], step[1]):
        pl.semaphore_signal(barrier, inc=1, device_id=target, device_id_type=MESH)

    def scaled(w_ref, s_ref, block, start):
        start = pl.multiple_of(start, cols)
        values = w_ref[block * BLOCK : (block + 1) * BLOCK, pl.ds(start, cols)]
        return (values.astype(jnp.float32) * s_ref[block : block + 1, pl.ds(start, cols)]).astype(
            jnp.bfloat16
        )

    def fill(dst, piece, owner):
        for block in range(width // BLOCK):
            low = block * BLOCK
            start = owner * units + piece * cols
            dst[piece, low : low + BLOCK, :cols] = scaled(wg_ref, sg_ref, block, start)
            dst[piece, low : low + BLOCK, cols:] = scaled(wu_ref, su_ref, block, start)

    def fill_down(dst, owner):
        for block in range(units // BLOCK):
            start = pl.multiple_of(owner * units + block * BLOCK, BLOCK)
            row = sd_ref[pl.ds(owner * (units // BLOCK) + block, 1), :]
            values = wd_ref[pl.ds(start, BLOCK), :].astype(jnp.float32) * row
            dst[block * BLOCK : (block + 1) * BLOCK, :] = values.astype(jnp.bfloat16)

    for piece in range(PIECES):
        fill(w_send, piece, 1 - side)
    pl.semaphore_wait(barrier, 3)
    send(x_ref, x_all.at[:, width:], x_sems, (0,), mate)
    for piece in range(PIECES):
        send(w_send.at[piece], w_all.at[piece, width:, :], w_sems, (piece,), mate)
    fill_down(d_send, 1 - side)
    send(d_send, d_far, w_sems, (PIECES,), mate)
    x_all[:, :width] = x_ref[...]
    for piece in range(PIECES):
        fill(w_all, piece, side)
    fill_down(d_own, side)
    remote(x_ref, x_all.at[:, width:], x_sems, (0,), mate).wait_recv()

    def rows_of(index):
        return pl.ds(pl.multiple_of(index * chunk, chunk), chunk)

    def runs(way, piece, hop):
        return 1 <= hop < half or (hop == half and piece // (PIECES // 2) == way)

    def wait_sum(way, hop, piece):
        remote(
            sum_out.at[way, hop - 1, piece],
            sum_in.at[way, hop - 1, piece],
            sum_sems,
            (way, hop - 1, piece),
            step[way],
        ).wait_recv()

    def wait_hidden(way, hop, part):
        origin = (z + ring - hop) % ring if way == 0 else (z + hop) % ring
        remote(
            hidden.at[origin, part],
            hidden.at[origin, part],
            gather_sems,
            (way, hop - 1, part),
            step[way],
        ).wait_recv()

    def gathers(way, part, hop):
        return 1 <= hop < half or (hop == half and part == way)

    arrived = set()

    def ready(way, hop, part):
        if (way, hop, part) not in arrived:
            arrived.add((way, hop, part))
            wait_hidden(way, hop, part)

    row_tile = rows // 3
    for _, _, kind, first, hop in schedule(half):
        if kind == "mul":
            piece = first
            remote(
                w_send.at[piece], w_all.at[piece, width:, :], w_sems, (piece,), mate
            ).wait_recv()
            for tile in range(3):
                low = tile * row_tile
                parts[piece, low : low + row_tile, :] = jnp.dot(
                    x_all[low : low + row_tile, :],
                    w_all[piece],
                    preferred_element_type=jnp.float32,
                )
        elif kind == "sum":
            piece = first
            for way in range(2):
                if not runs(way, piece, hop):
                    continue
                owner = (z + hop) % ring if way == 0 else (z + ring - hop) % ring
                total = parts[piece, rows_of(owner), :]
                if runs(way, piece, hop + 1):
                    wait_sum(way, hop + 1, piece)
                    total = total + sum_in[way, hop, piece].astype(jnp.float32)
                sum_out[way, hop - 1, piece] = total.astype(jnp.bfloat16)
                send(
                    sum_out.at[way, hop - 1, piece],
                    sum_in.at[way, hop - 1, piece],
                    sum_sems,
                    (way, hop - 1, piece),
                    step[way],
                )
        elif kind == "act":
            piece = first
            total = parts[piece, rows_of(z), :]
            for way in range(2):
                wait_sum(way, 1, piece)
                total = total + sum_in[way, 0, piece].astype(jnp.float32)
            gate = total[:, :cols]
            act = gate / (1.0 + jnp.exp(-gate)) * total[:, cols:]
            low = (piece % 2) * cols
            hidden[z, piece // 2, :, low : low + cols] = act.astype(jnp.bfloat16)
        elif kind == "gather":
            part = first
            for way in range(2):
                if not gathers(way, part, hop):
                    continue
                if hop > 1:
                    ready(way, hop - 1, part)
                origin = (z + ring - hop + 1) % ring if way == 0 else (z + hop - 1) % ring
                send(
                    hidden.at[origin, part],
                    hidden.at[origin, part],
                    gather_sems,
                    (way, hop - 1, part),
                    step[way],
                )
        else:
            if hop == 0:
                remote(d_send, d_far, w_sems, (PIECES,), mate).wait_recv()
                todo = ((0, z),)
            elif hop < half:
                todo = ((2 * hop - 1, (z + ring - hop) % ring), (2 * hop, (z + hop) % ring))
            else:
                todo = ((ring - 1, (z + half) % ring),)
            if hop > 0:
                for way in range(2):
                    for part in range(2):
                        if gathers(way, part, hop):
                            ready(way, hop, part)
            for slot, origin in todo:
                own = jnp.zeros((chunk, width), jnp.float32)
                far = jnp.zeros((chunk, width), jnp.float32)
                for part in range(2):
                    low = part * (units // 2)
                    lhs = hidden[origin, part]
                    own = own + jnp.dot(
                        lhs, d_own[low : low + units // 2, :], preferred_element_type=jnp.float32
                    )
                    far = far + jnp.dot(
                        lhs, d_far[low : low + units // 2, :], preferred_element_type=jnp.float32
                    )
                y_own[slot] = own
                y_out[slot] = far.astype(jnp.bfloat16)
                send(y_out.at[slot], y_in.at[slot], y_sems, (slot,), mate)

    for slot in range(ring):
        if slot == 0:
            origin = z
        elif slot == ring - 1:
            origin = (z + half) % ring
        elif slot % 2 == 1:
            origin = (z + ring - (slot + 1) // 2) % ring
        else:
            origin = (z + slot // 2) % ring
        remote(y_out.at[slot], y_in.at[slot], y_sems, (slot,), mate).wait_recv()
        out_ref[rows_of(origin), :] = (
            y_own[slot] + y_in[slot].astype(jnp.float32)
        ).astype(jnp.bfloat16)
    for copy in sends:
        copy.wait_send()


def expert_call(incoming, w_gate, w_up, w_down, s_gate, s_up, s_down, ring):
    rows, width = incoming.shape
    units = w_gate.shape[1] // 2
    cols = units // PIECES
    half = ring // 2
    chunk = rows // ring
    vmem = pl.BlockSpec(memory_space=pltpu.VMEM)
    bf16, f32 = jnp.bfloat16, jnp.float32
    return pl.pallas_call(
        functools.partial(expert_kernel, ring),
        out_shape=jax.ShapeDtypeStruct((rows, width), bf16),
        in_specs=[vmem] * 7,
        out_specs=vmem,
        scratch_shapes=[
            pltpu.VMEM((rows, 2 * width), bf16),
            pltpu.VMEM((PIECES, width, 2 * cols), bf16),
            pltpu.VMEM((PIECES, 2 * width, 2 * cols), bf16),
            pltpu.VMEM((units, width), bf16),
            pltpu.VMEM((units, width), bf16),
            pltpu.VMEM((units, width), bf16),
            pltpu.VMEM((PIECES, rows, 2 * cols), f32),
            pltpu.VMEM((2, half, PIECES, chunk, 2 * cols), bf16),
            pltpu.VMEM((2, half, PIECES, chunk, 2 * cols), bf16),
            pltpu.VMEM((ring, 2, chunk, units // 2), bf16),
            pltpu.VMEM((ring, chunk, width), f32),
            pltpu.VMEM((ring, chunk, width), bf16),
            pltpu.VMEM((ring, chunk, width), bf16),
            pltpu.SemaphoreType.DMA((2, 1)),
            pltpu.SemaphoreType.DMA((2, PIECES + 1)),
            pltpu.SemaphoreType.DMA((2, 2, half, PIECES)),
            pltpu.SemaphoreType.DMA((2, 2, half, 2)),
            pltpu.SemaphoreType.DMA((2, ring)),
        ],
        compiler_params=pltpu.CompilerParams(collective_id=0, has_side_effects=True),
        name="expert_layer",
    )(incoming, w_gate, w_up, w_down, s_gate, s_up, s_down)


def shards(tokens, expert_ids, gate_values, w_gate, w_up, w_down, scale_gate, scale_up, scale_down):
    device_count = lax.axis_size("expert")
    ring = lax.axis_size("fsdp") // 2
    slices = device_count // EXPERTS
    local_tokens = tokens.shape[0]
    feature_cols = tokens.shape[1]
    slot_total = EXPERTS * CAP
    flat_ids = expert_ids.reshape(-1)
    onehot = (flat_ids[:, None] == jnp.arange(EXPERTS, dtype=jnp.int32)[None, :]).astype(jnp.int32)
    slot_rank = jnp.sum((jnp.cumsum(onehot, axis=0) - onehot) * onehot, axis=1)
    target = flat_ids * CAP + slot_rank
    placing = (target[:, None] == jnp.arange(slot_total, dtype=jnp.int32)[None, :]).astype(
        jnp.float32
    )
    token_map = jnp.sum(placing.reshape(local_tokens, 2, slot_total), axis=1).astype(jnp.bfloat16)
    packed = jnp.einsum("ts,td->sd", token_map, tokens, preferred_element_type=jnp.float32).astype(
        jnp.bfloat16
    )
    outgoing = jnp.broadcast_to(
        packed.reshape(EXPERTS, 1, CAP, feature_cols), (EXPERTS, slices, CAP, feature_cols)
    ).reshape(device_count * CAP, feature_cols)
    incoming = lax.all_to_all(outgoing, "expert", split_axis=0, concat_axis=0, tiled=True)
    partial_rows = expert_call(
        incoming,
        w_gate,
        w_up,
        w_down,
        jnp.repeat(scale_gate, BLOCK, axis=1),
        jnp.repeat(scale_up, BLOCK, axis=1),
        jnp.repeat(scale_down, BLOCK, axis=1),
        ring,
    )
    returned = lax.all_to_all(partial_rows, "expert", split_axis=0, concat_axis=0, tiled=True)
    slice_sums = jnp.sum(
        returned.reshape(EXPERTS, slices, CAP, feature_cols).astype(jnp.float32), axis=1
    )
    slice_sums = slice_sums.reshape(slot_total, feature_cols)
    weights_map = jnp.sum(
        (placing * gate_values.reshape(-1)[:, None]).reshape(local_tokens, 2, slot_total), axis=1
    )
    mixed_rows = jnp.dot(
        weights_map, slice_sums, precision=lax.Precision.HIGHEST, preferred_element_type=jnp.float32
    )
    return mixed_rows.astype(jnp.bfloat16)


def solution(mesh):
    in_specs = (
        P("expert", "fsdp"),
        P("expert", None),
        P("expert", None),
        P("fsdp", "expert"),
        P("fsdp", "expert"),
        P("expert", "fsdp"),
        P("fsdp", "expert"),
        P("fsdp", "expert"),
        P("expert", "fsdp"),
    )
    out_specs = P("expert", "fsdp")
    return jax.shard_map(shards, mesh=mesh, in_specs=in_specs, out_specs=out_specs, check_vma=False)
```

time: 421 us -> 164 us (0.39)
  waiting for transfers between devices: 318 us -> 13.5 us
  Pallas kernels: 0 us -> 97.1 us
  blocking collectives: 69.3 us -> 30.6 us
  starting transfers between devices: 0.09 us -> 14.1 us
  between operations: 13.2 us -> 0.1 us
  matrix products: 7.79 us -> 1.04 us
    reduce_scatter x2 -> x0, waiting for transfers between devices: 208 us -> none  [the longest x1 115 us: shards(): lax.psum_scatter(make_term(dequant(w_gate, scale_gate)).astype(jnp.bfloat...]
    all_gather x1 -> x0, waiting for transfers between devices: 110 us -> none  [shards(): lax.all_gather(hidden, 'fsdp', axis=0, tiled=True)]
    pallas_call x0 -> x1, Pallas kernels: none -> 97.1 us  [expert_call(): pl.pallas_call(functools.partial(expert_kernel, ring), out_shape=jax.Shap...]
    all_to_all x1 -> x0, blocking collectives: 28.8 us -> none  [shards(): lax.all_to_all(outgoing, 'expert', split_axis=0, concat_axis=0, tiled=True)]
    all_to_all x0 -> x1, starting transfers between devices: none -> 14.1 us  [shards(): lax.all_to_all(outgoing, 'expert', split_axis=0, concat_axis=0, tiled=True)]
    all_to_all x0 -> x1, waiting for transfers between devices: none -> 13.5 us  [shards(): lax.all_to_all(outgoing, 'expert', split_axis=0, concat_axis=0, tiled=True)]
    all_to_all x1, blocking collectives: 40.5 us -> 30.6 us  [shards(): lax.all_to_all(partial_rows, 'expert', split_axis=0, concat_axis=0, tiled...]
    dot_general x3 -> x0, matrix products: 6.74 us -> none  [the longest x2 5.7 us: make_term(): jnp.dot(incoming, weights, preferred_element_type=jnp.float32)]
  transfers between devices with their start and end apart: 3 -> 1, of which waited for: 3 -> 1; matrix products, arithmetic and copies ran while one was open for 1% -> 1% of each run, Pallas kernels for 0% -> 0%
where the time goes in v1:
time: 164 us; the launch traced here: 163 us
  Pallas kernels  97.1 us (59%)
  blocking collectives  30.6 us (19%)
  starting transfers between devices  14.1 us (9%)
  waiting for transfers between devices  13.5 us (8%)
  local copies, waits for them, and re-layouts  6.13 us (4%)
    pallas_call x1, Pallas kernels, expert_call(): pl.pallas_call(functools.partial(expert_kernel, ring), out_shape=jax.Shap...  97.1 us
    all_to_all x1, blocking collectives, shards(): lax.all_to_all(partial_rows, 'expert', split_axis=0, concat_axis=0, tiled...  30.6 us
    all_to_all x1, starting transfers between devices, shards(): lax.all_to_all(outgoing, 'expert', split_axis=0, concat_axis=0, tiled=True)  14.1 us
    all_to_all x1, waiting for transfers between devices, shards(): lax.all_to_all(outgoing, 'expert', split_axis=0, concat_axis=0, tiled=True)  13.5 us
    unnamed x19, local copies, waits for them, and re-layouts  4.32 us
  transfers between devices with their start and end apart: 1, of which 1 were waited for; matrix products, arithmetic and copies ran while one was open for 1% of the time, Pallas kernels for 0%

profile of v1, /device:TPU:1, one launch (start us, length us, event | category | flops | bytes accessed | tf_op | source)
XLA Modules:
  0.0 163.1 jit_solution(15278029945054022420)
XLA Ops:
  0.0 0.0 copy-start
  0.0 0.8 copy.25
  0.8 0.1 eq.30
  0.9 0.1 fusion
  1.0 0.2 reduce_window_sum.11
  1.2 0.2 select_reduce_fusion.1
  1.4 0.1 reduce_sum.39
  1.5 0.0 copy-start.2
  1.5 0.1 copy.26
  1.6 0.6 copy-done.2
  2.2 0.0 copy-start.3
  2.2 0.7 copy-done.3
  2.9 0.1 convert_reduce_fusion.1
  3.0 0.0 copy-done
  3.0 0.2 convolution_convert_fusion
  3.2 0.8 broadcast_in_dim.20
  4.0 14.1 %all-to-all-start = ((bf16[32,24,256]{2,1,0:T(8,128)(2,1)}), bf16[32,24,256]{2,1,0:T(8,128)(2,1)S(1)}, u32[]{:S(2)}, u32[]{:S(2)}) async-start(bf16[32,24,256]{2,1,0:T(8,128)(2,1)} %bitcast.1), calls=%async_computation | async-start | bytes 786432 | tf_op jit(solution)/shard_map/all_to_all | solution.py:333
  18.1 0.0 copy-done.4
  18.1 0.0 copy-start.5
  18.1 0.1 broadcast_bitcast_fusion
  18.2 0.6 copy-done.5
  18.8 0.1 copy.27
  18.9 0.1 broadcast_in_dim.23
  19.0 0.6 copy.34
  19.6 0.1 copy-done.6
  19.7 0.1 broadcast_bitcast_fusion.1
  19.7 0.6 copy_bitcast_fusion.1
  20.4 13.5 %all-to-all-done = bf16[32,24,256]{2,1,0:T(8,128)(2,1)S(1)} async-done(((bf16[32,24,256]{2,1,0:T(8,128)(2,1)}), bf16[32,24,256]{2,1,0:T(8,128)(2,1)S(1)}, u32[]{:S(2)}, u32[]{:S(2)}) %all-to-all-start) | async-done | bytes 393248 | tf_op jit(solution)/shard_map/all_to_all | solution.py:333
  33.8 0.7 copy-done.1
  34.5 97.1 %expert_layer.1 = bf16[768,256]{1,0:T(8,128)(2,1)} custom-call(bf16[768,256]{1,0:T(8,128)(2,1)} %bitcast.24, bf16[256,2048]{1,0:T(8,128)(2,1)} %wg_ref.1, bf16[256,2048]{1,0:T(8,128)(2,1)} %wu_ref.1, bf16[2048,256]{1,0:T(8,128)(2,1)} %wd_ref.1, f32[2,2048]{1,0:T(2,128)} %get-tuple-element.8.sg_ref, f32[2,2048]{1,0:T(2,128)} %get-tuple-element.7.su_ref, ...), custom_call_target="tpu_custom_call" | custom-call | tf_op jit(solution)/shard_map/expert_layer/pallas_call | solution.py:282
  131.6 30.6 %all_to_all.20 = bf16[32,24,256]{2,1,0:T(8,128)(2,1)S(1)} all-to-all(bf16[32,24,256]{2,1,0:T(8,128)(2,1)} %bitcast.25), channel_id=1, replica_groups=mesh['fsdp'=24,'expert'=32] {'expert'}, dimensions={0} | all-to-all | bytes 786432 | tf_op jit(solution)/shard_map/all_to_all | solution.py:344
  162.3 0.8 convolution_convert_fusion.1
  (5 shorter events, 0.1 us)
Async XLA Ops:
  0.0 3.0 %copy-start = (bf16[64,256]{1,0:T(8,128)(2,1)S(1)}, bf16[64,256]{1,0:T(8,128)(2,1)}, u32[]{:S(2)}) copy-start(bf16[64,256]{1,0:T(8,128)(2,1)} %param.9) | copy-start | bytes 98308
  1.5 0.7 copy-start.2
  2.2 0.7 copy-start.3
  4.0 14.2 %copy-start.4 = (f32[2,16]{1,0:T(2,128)S(1)}, f32[2,16]{1,0:T(2,128)}, u32[]{:S(2)}) copy-start(f32[2,16]{1,0:T(2,128)} %param.16) | copy-start | bytes 388
  4.0 29.8 %all-to-all-start = ((bf16[32,24,256]{2,1,0:T(8,128)(2,1)}), bf16[32,24,256]{2,1,0:T(8,128)(2,1)S(1)}, u32[]{:S(2)}, u32[]{:S(2)}) async-start(bf16[32,24,256]{2,1,0:T(8,128)(2,1)} %bitcast.1), calls=%async_computation | async-start | bytes 786432 | tf_op jit(solution)/shard_map/all_to_all | solution.py:333
  18.1 0.7 copy-start.5
  19.0 0.7 copy-start.6
  33.8 0.7 copy-start.1

commit v2 on v1

v2 whole, which is shorter than its diff:
```python
import functools

import jax
import jax.numpy as jnp
from jax import lax
from jax.experimental import pallas as pl
from jax.experimental.pallas import tpu as pltpu
from jax.sharding import PartitionSpec as P

EXPERTS = 8
BLOCK = 128
CAP = 24
PIECES = 4
OFFSETS = (0, 0, 2, 4)
MESH = pl.DeviceIdType.MESH


def schedule(half):
    tasks = []
    for piece in range(PIECES):
        begin = OFFSETS[piece]
        tasks.append((begin - 0.5, 0, "mul", piece, 0))
        for hop in range(half, 0, -1):
            tasks.append((begin + half - hop, 1, "sum", piece, hop))
        tasks.append((begin + half, 2, "act", piece, 0))
    for part in range(2):
        begin = max(OFFSETS[2 * part], OFFSETS[2 * part + 1]) + half
        for hop in range(1, half + 1):
            tasks.append((begin + hop - 0.5, 3, "gather", part, hop))
    begin = max(OFFSETS) + half
    tasks.append((begin + 0.6, 4, "down", 0, 0))
    for hop in range(1, half + 1):
        tasks.append((begin + hop + 0.6, 4, "down", 0, hop))
    for hop in range(half + 1):
        tasks.append((begin + hop + 1.7, 5, "back", 0, hop))
    return sorted(tasks)


def expert_kernel(
    ring,
    idc_ref,
    idr_ref,
    gv_ref,
    tok_ref,
    wg_ref,
    wu_ref,
    wd_ref,
    sg_ref,
    su_ref,
    sd_ref,
    out_ref,
    packed,
    x_near,
    x_far,
    x_all,
    w_send,
    w_all,
    d_send,
    d_own,
    d_far,
    parts,
    sum_out,
    sum_in,
    hidden,
    y_own,
    y_out,
    y_in,
    y_back,
    landed,
    route_sems,
    mate_sems,
    near_sems,
    far_sems,
    w_sems,
    sum_sems,
    gather_sems,
    y_sems,
    back_sems,
):
    half = ring // 2
    local_tokens, width = tok_ref.shape
    rows = x_all.shape[0]
    chunk = rows // ring
    units = wg_ref.shape[1] // 2
    cols = units // PIECES
    slots = EXPERTS * CAP
    place = lax.axis_index("fsdp")
    z = place // 2
    side = place % 2
    seat = lax.axis_index("expert")
    high = seat // 16
    y = (seat // 2) % 8
    core = seat % 2
    expert = high * 4 + y // 2
    share = (y % 2) * 2 + core
    mate = {"fsdp": z * 2 + (1 - side)}
    sibling = {"expert": seat + 1 - 2 * core}
    step = {
        0: {"fsdp": ((z + 1) % ring) * 2 + side},
        1: {"fsdp": ((z + ring - 1) % ring) * 2 + side},
    }
    sends = []

    def remote(src, dst, sems, index, target):
        return pltpu.make_async_remote_copy(
            src_ref=src,
            dst_ref=dst,
            send_sem=sems.at[(0,) + index],
            recv_sem=sems.at[(1,) + index],
            device_id=target,
            device_id_type=MESH,
        )

    def send(*args):
        copy = remote(*args)
        copy.start()
        sends.append(copy)

    barrier = pltpu.get_barrier_semaphore()
    for target in (mate, step[0], step[1]):
        pl.semaphore_signal(barrier, inc=1, device_id=target, device_id_type=MESH)
    for other in range(1, 32):
        target = {"expert": (seat + other) % 32}
        pl.semaphore_signal(barrier, inc=1, device_id=target, device_id_type=MESH)

    def scaled(w_ref, s_ref, block, start):
        tiles = []
        for lane in range(cols // BLOCK):
            low = pl.multiple_of(start + lane * BLOCK, BLOCK)
            values = w_ref[block * BLOCK : (block + 1) * BLOCK, pl.ds(low, BLOCK)]
            scale = s_ref[block, start // BLOCK + lane]
            tiles.append((values.astype(jnp.float32) * scale).astype(jnp.bfloat16))
        return tiles

    def fill(dst, piece, owner):
        for block in range(width // BLOCK):
            low = block * BLOCK
            start = owner * units + piece * cols
            for index, (w_ref, s_ref) in enumerate(((wg_ref, sg_ref), (wu_ref, su_ref))):
                for lane, tile in enumerate(scaled(w_ref, s_ref, block, start)):
                    left = index * cols + lane * BLOCK
                    dst[piece, low : low + BLOCK, left : left + BLOCK] = tile

    def fill_down(dst, owner):
        for block in range(units // BLOCK):
            start = pl.multiple_of(owner * units + block * BLOCK, BLOCK)
            for lane in range(width // BLOCK):
                left = lane * BLOCK
                scale = sd_ref[owner * (units // BLOCK) + block, lane]
                values = wd_ref[pl.ds(start, BLOCK), left : left + BLOCK].astype(jnp.float32)
                dst[block * BLOCK : (block + 1) * BLOCK, left : left + BLOCK] = (
                    values * scale
                ).astype(jnp.bfloat16)

    def iota(shape, axis):
        return lax.broadcasted_iota(jnp.int32, shape, axis)

    def mask(test, kind):
        return jnp.where(test, 1.0, 0.0).astype(kind)

    square = (local_tokens, local_tokens)
    names = iota((EXPERTS, local_tokens), 0)
    picks = [mask(names == idr_ref[k : k + 1, :], jnp.float32) for k in range(2)]
    before = jnp.dot(
        (picks[0] + picks[1]).astype(jnp.bfloat16),
        mask(iota(square, 0) < iota(square, 1), jnp.bfloat16),
        preferred_element_type=jnp.float32,
    )
    spots = iota((slots, local_tokens), 0)
    chosen = jnp.zeros((slots, local_tokens), jnp.float32)
    for k in range(2):
        rank = jnp.sum(before * picks[k], axis=0, keepdims=True).astype(jnp.int32)
        chosen = chosen + mask(spots == idr_ref[k : k + 1, :] * CAP + rank, jnp.float32)
    picked = jnp.dot(
        chosen.astype(jnp.bfloat16), tok_ref[...], preferred_element_type=jnp.float32
    )
    packed[...] = picked.reshape(packed.shape).astype(jnp.bfloat16)

    fill(w_send, 0, 1 - side)
    pl.semaphore_wait(barrier, 34)
    my_block = core * 2 + high

    def block_of(turn):
        return core * 2 + (high + turn) % 2

    def send_piece(piece):
        send(w_send.at[piece], w_all.at[piece, width:, :], w_sems, (piece,), mate)

    def wait_bytes(ref, sem):
        pltpu.make_async_copy(ref, ref, sem).wait()

    for turn in range(2):
        for other in (4, 3, 5, 2, 6, 1, 7, 0):
            to_high = (high + turn) % 2
            to_y = (y + other) % 8
            src = packed.at[to_high * 4 + to_y // 2]
            dst = x_near.at[my_block, :, y]
            if turn == 0 and other == 0:
                pltpu.make_async_copy(src, dst, route_sems.at[1, 0]).start()
            else:
                target = {"expert": to_high * 16 + to_y * 2 + core}
                remote(src, dst, route_sems, (turn,), target).start()
    send_piece(0)
    for piece in range(1, PIECES):
        fill(w_send, piece, 1 - side)
    for piece in range(PIECES):
        fill(w_all, piece, side)
    for turn in range(2):
        block = block_of(turn)
        wait_bytes(x_near.at[block], route_sems.at[1, turn])
        send(x_near.at[block], x_far.at[block], mate_sems, (turn,), mate)
        send(x_near.at[block], x_near.at[block], near_sems, (turn,), sibling)
    for piece in range(1, PIECES):
        send_piece(piece)
    fill_down(d_send, 1 - side)
    send(d_send, d_far, w_sems, (PIECES,), mate)
    for turn in range(2):
        block = block_of(turn)
        remote(x_near.at[block], x_far.at[block], mate_sems, (turn,), mate).wait_recv()
        send(x_far.at[block], x_far.at[block], far_sems, (turn,), sibling)
    fill_down(d_own, side)
    for turn in range(2):
        block = (1 - core) * 2 + (high + turn) % 2
        remote(x_near.at[block], x_near.at[block], near_sems, (turn,), sibling).wait_recv()
        remote(x_far.at[block], x_far.at[block], far_sems, (turn,), sibling).wait_recv()
    part_rows = rows // 4
    for block in range(4):
        for index, source in enumerate((x_near, x_far)):
            values = source[block].astype(jnp.float32).reshape(part_rows, width)
            x_all[
                block * part_rows : (block + 1) * part_rows, index * width : (index + 1) * width
            ] = values.astype(jnp.bfloat16)

    def rows_of(index):
        return pl.ds(pl.multiple_of(index * chunk, chunk), chunk)

    def runs(way, piece, hop):
        return 1 <= hop < half or (hop == half and piece // (PIECES // 2) == way)

    def wait_sum(way, hop, piece):
        remote(
            sum_out.at[way, hop - 1, piece],
            sum_in.at[way, hop - 1, piece],
            sum_sems,
            (way, hop - 1, piece),
            step[way],
        ).wait_recv()

    def wait_hidden(way, hop, part):
        origin = (z + ring - hop) % ring if way == 0 else (z + hop) % ring
        remote(
            hidden.at[origin, part],
            hidden.at[origin, part],
            gather_sems,
            (way, hop - 1, part),
            step[way],
        ).wait_recv()

    def gathers(way, part, hop):
        return 1 <= hop < half or (hop == half and part == way)

    arrived = set()

    def ready(way, hop, part):
        if (way, hop, part) not in arrived:
            arrived.add((way, hop, part))
            wait_hidden(way, hop, part)

    def chunks_at(hop):
        if hop == 0:
            return ((0, z),)
        if hop < half:
            return ((2 * hop - 1, (z + ring - hop) % ring), (2 * hop, (z + hop) % ring))
        return ((ring - 1, (z + half) % ring),)

    row_tile = rows // 3
    for _, _, kind, first, hop in schedule(half):
        if kind == "mul":
            piece = first
            remote(
                w_send.at[piece], w_all.at[piece, width:, :], w_sems, (piece,), mate
            ).wait_recv()
            for tile in range(3):
                low = tile * row_tile
                parts[piece, low : low + row_tile, :] = jnp.dot(
                    x_all[low : low + row_tile, :],
                    w_all[piece],
                    preferred_element_type=jnp.float32,
                )
        elif kind == "sum":
            piece = first
            for way in range(2):
                if not runs(way, piece, hop):
                    continue
                owner = (z + hop) % ring if way == 0 else (z + ring - hop) % ring
                total = parts[piece, rows_of(owner), :]
                if runs(way, piece, hop + 1):
                    wait_sum(way, hop + 1, piece)
                    total = total + sum_in[way, hop, piece].astype(jnp.float32)
                sum_out[way, hop - 1, piece] = total.astype(jnp.bfloat16)
                send(
                    sum_out.at[way, hop - 1, piece],
                    sum_in.at[way, hop - 1, piece],
                    sum_sems,
                    (way, hop - 1, piece),
                    step[way],
                )
        elif kind == "act":
            piece = first
            total = parts[piece, rows_of(z), :]
            for way in range(2):
                wait_sum(way, 1, piece)
                total = total + sum_in[way, 0, piece].astype(jnp.float32)
            gate = total[:, :cols]
            act = gate / (1.0 + jnp.exp(-gate)) * total[:, cols:]
            low = (piece % 2) * cols
            hidden[z, piece // 2, :, low : low + cols] = act.astype(jnp.bfloat16)
        elif kind == "gather":
            part = first
            for way in range(2):
                if not gathers(way, part, hop):
                    continue
                if hop > 1:
                    ready(way, hop - 1, part)
                origin = (z + ring - hop + 1) % ring if way == 0 else (z + hop - 1) % ring
                send(
                    hidden.at[origin, part],
                    hidden.at[origin, part],
                    gather_sems,
                    (way, hop - 1, part),
                    step[way],
                )
        elif kind == "down":
            if hop == 0:
                remote(d_send, d_far, w_sems, (PIECES,), mate).wait_recv()
            else:
                for way in range(2):
                    for part in range(2):
                        if gathers(way, part, hop):
                            ready(way, hop, part)
            for slot, origin in chunks_at(hop):
                own = jnp.zeros((chunk, width), jnp.float32)
                far = jnp.zeros((chunk, width), jnp.float32)
                for part in range(2):
                    low = part * (units // 2)
                    lhs = hidden[origin, part]
                    far = far + jnp.dot(
                        lhs, d_far[low : low + units // 2, :], preferred_element_type=jnp.float32
                    )
                    own = own + jnp.dot(
                        lhs, d_own[low : low + units // 2, :], preferred_element_type=jnp.float32
                    )
                y_own[slot] = own
                y_out[slot] = far.astype(jnp.bfloat16)
                send(y_out.at[slot], y_in.at[slot], y_sems, (slot,), mate)
        else:
            for slot, origin in chunks_at(hop):
                remote(y_out.at[slot], y_in.at[slot], y_sems, (slot,), mate).wait_recv()
                total = y_own[slot] + y_in[slot].astype(jnp.float32)
                y_back[slot * 8 : slot * 8 + 8] = total.reshape(8, 8, width).astype(jnp.bfloat16)
                block = origin // 3
                dst = landed.at[share, expert, origin % 3]
                for other in range(8):
                    to_y = (y + other) % 8
                    src = y_back.at[slot * 8 + to_y]
                    target = {"expert": (block % 2) * 16 + to_y * 2 + block // 2}
                    copy = remote(src, dst, back_sems, (), target)
                    if other > 0:
                        copy.start()
                    else:
                        pl.when(block != my_block)(copy.start)
                        pl.when(block == my_block)(
                            pltpu.make_async_copy(src, dst, back_sems.at[1]).start
                        )

    lanes = iota((local_tokens, BLOCK), 1)
    picks = [mask(lanes == idc_ref[:, k : k + 1], jnp.float32) for k in range(2)]
    before = jnp.dot(
        mask(iota(square, 1) < iota(square, 0), jnp.bfloat16),
        (picks[0] + picks[1]).astype(jnp.bfloat16),
        preferred_element_type=jnp.float32,
    )
    spots = iota((local_tokens, slots), 1)
    mixing = jnp.zeros((local_tokens, slots), jnp.float32)
    for k in range(2):
        rank = jnp.sum(before * picks[k], axis=1, keepdims=True).astype(jnp.int32)
        found = spots == idc_ref[:, k : k + 1] * CAP + rank
        mixing = mixing + jnp.where(found, gv_ref[:, k : k + 1], 0.0)
    wait_bytes(landed, back_sems.at[1])
    sums = landed[0].astype(jnp.float32)
    for index in range(1, 4):
        sums = sums + landed[index].astype(jnp.float32)
    out_ref[...] = jnp.dot(
        mixing,
        sums.reshape(slots, width),
        precision=lax.Precision.HIGHEST,
        preferred_element_type=jnp.float32,
    ).astype(jnp.bfloat16)

    wait_bytes(packed.at[:7], route_sems.at[0, 0])
    wait_bytes(packed, route_sems.at[0, 1])
    wait_bytes(y_back.at[:93], back_sems.at[0])
    for copy in sends:
        copy.wait_send()


def shards(tokens, expert_ids, gate_values, w_gate, w_up, w_down, scale_gate, scale_up, scale_down):
    ring = lax.axis_size("fsdp") // 2
    local_tokens, width = tokens.shape
    rows = lax.axis_size("expert") * CAP
    units = w_gate.shape[1] // 2
    cols = units // PIECES
    half = ring // 2
    chunk = rows // ring
    vmem = pl.BlockSpec(memory_space=pltpu.VMEM)
    smem = pl.BlockSpec(memory_space=pltpu.SMEM)
    bf16, f32 = jnp.bfloat16, jnp.float32
    dma = pltpu.SemaphoreType.DMA
    return pl.pallas_call(
        functools.partial(expert_kernel, ring),
        out_shape=jax.ShapeDtypeStruct((local_tokens, width), bf16),
        in_specs=[vmem] * 7 + [smem] * 3,
        out_specs=vmem,
        scratch_shapes=[
            pltpu.VMEM((EXPERTS, 3, 8, width), bf16),
            pltpu.VMEM((4, 3, 8, 8, width), bf16),
            pltpu.VMEM((4, 3, 8, 8, width), bf16),
            pltpu.VMEM((rows, 2 * width), bf16),
            pltpu.VMEM((PIECES, width, 2 * cols), bf16),
            pltpu.VMEM((PIECES, 2 * width, 2 * cols), bf16),
            pltpu.VMEM((units, width), bf16),
            pltpu.VMEM((units, width), bf16),
            pltpu.VMEM((units, width), bf16),
            pltpu.VMEM((PIECES, rows, 2 * cols), f32),
            pltpu.VMEM((2, half, PIECES, chunk, 2 * cols), bf16),
            pltpu.VMEM((2, half, PIECES, chunk, 2 * cols), bf16),
            pltpu.VMEM((ring, 2, chunk, units // 2), bf16),
            pltpu.VMEM((ring, chunk, width), f32),
            pltpu.VMEM((ring, chunk, width), bf16),
            pltpu.VMEM((ring, chunk, width), bf16),
            pltpu.VMEM((ring * 8, 8, width), bf16),
            pltpu.VMEM((4, EXPERTS, 3, 8, width), bf16),
            dma((2, 2)),
            dma((2, 2)),
            dma((2, 2)),
            dma((2, 2)),
            dma((2, PIECES + 1)),
            dma((2, 2, half, PIECES)),
            dma((2, 2, half, 2)),
            dma((2, ring)),
            dma((2,)),
        ],
        compiler_params=pltpu.CompilerParams(collective_id=0, has_side_effects=True),
        name="expert_layer",
    )(
        expert_ids,
        expert_ids.T,
        gate_values,
        tokens,
        w_gate,
        w_up,
        w_down,
        scale_gate,
        scale_up,
        scale_down,
    )


def solution(mesh):
    in_specs = (
        P("expert", "fsdp"),
        P("expert", None),
        P("expert", None),
        P("fsdp", "expert"),
        P("fsdp", "expert"),
        P("expert", "fsdp"),
        P("fsdp", "expert"),
        P("fsdp", "expert"),
        P("expert", "fsdp"),
    )
    out_specs = P("expert", "fsdp")
    return jax.shard_map(shards, mesh=mesh, in_specs=in_specs, out_specs=out_specs, check_vma=False)
```

time: 164 us -> 126 us (0.77)
  blocking collectives: 30.6 us -> 0 us
  Pallas kernels: 97.1 us -> 122 us
  starting transfers between devices: 14.1 us -> 0 us
  waiting for transfers between devices: 13.5 us -> 0 us
  local copies, waits for them, and re-layouts: 6.13 us -> 4.16 us
    all_to_all x1 -> x0, blocking collectives: 30.6 us -> none  [shards(): lax.all_to_all(partial_rows, 'expert', split_axis=0, concat_axis=0, tiled...]
    pallas_call x1, Pallas kernels: 97.1 us -> 122 us  [shards(): pl.pallas_call(functools.partial(expert_kernel, ring), out_shape=jax.Shap...]
    all_to_all x1 -> x0, starting transfers between devices: 14.1 us -> none  [shards(): lax.all_to_all(outgoing, 'expert', split_axis=0, concat_axis=0, tiled=True)]
    all_to_all x1 -> x0, waiting for transfers between devices: 13.5 us -> none  [shards(): lax.all_to_all(outgoing, 'expert', split_axis=0, concat_axis=0, tiled=True)]
    unnamed x19 -> x10, local copies, waits for them, and re-layouts: 4.32 us -> 4.16 us
  transfers between devices with their start and end apart: 1 -> 0, of which waited for: 1 -> 0; matrix products, arithmetic and copies ran while one was open for 1% -> 0% of each run, Pallas kernels for 0% -> 0%
where the time goes in v2:
time: 126 us
  Pallas kernels  122 us (97%)
  local copies, waits for them, and re-layouts  4.16 us (3%)
    pallas_call x1, Pallas kernels, shards(): pl.pallas_call(functools.partial(expert_kernel, ring), out_shape=jax.Shap...  122 us
    unnamed x10, local copies, waits for them, and re-layouts  4.16 us

profile of v2, /device:TPU:1, one launch (start us, length us, event | category | flops | bytes accessed | tf_op | source)
XLA Modules:
  0.0 126.1 jit_solution(2034602823078651668)
XLA Ops:
  0.0 0.0 copy-start.1
  0.0 0.7 copy-done.1
  0.7 0.0 copy-start.2
  0.7 0.7 copy.12.sd_ref
  1.4 0.0 copy-done.2
  1.4 0.0 copy-start
  1.4 0.7 copy.11.gv_ref
  2.1 0.0 copy-done
  2.1 0.7 copy.10.idc_ref
  2.8 121.9 %expert_layer.1 = bf16[64,256]{1,0:T(8,128)(2,1)} custom-call(s32[64,2]{1,0:T(8,128)} %copy.10.idc_ref, s32[2,64]{1,0:T(2,128)} %bitcast.1, f32[64,2]{1,0:T(8,128)} %copy.11.gv_ref, bf16[64,256]{1,0:T(8,128)(2,1)} %tok_ref.1, bf16[256,2048]{1,0:T(8,128)(2,1)} %wg_ref.1, bf16[256,2048]{1,0:T(8,128)(2,1)} %wu_ref.1, bf16[2048,256]{1,0:T(8,128)(2,1)} %wd_ref.1, ...), custom_call_target="tpu_custom_call" | custom-call | tf_op jit(solution)/shard_map/expert_layer/pallas_call | solution.py:419
  124.7 1.4 %copy.14 = bf16[64,256]{1,0:T(8,128)(2,1)} copy(bf16[64,256]{1,0:T(8,128)(2,1)} %expert_layer.1) | data formatting | bytes 65536
Async XLA Ops:
  0.0 0.7 copy-start.1
  0.7 0.7 copy-start.2
  1.4 0.7 copy-start

commit v3 on v2

v3 whole, which is shorter than its diff:
```python
import functools

import jax
import jax.numpy as jnp
from jax import lax
from jax.experimental import pallas as pl
from jax.experimental.pallas import tpu as pltpu
from jax.sharding import PartitionSpec as P

EXPERTS = 8
BLOCK = 128
CAP = 24
PIECES = 8
PARTS = 4
FIRST = 2
X_AT = 19.0
W_AT = (8.0, 11.0, 18.5, 21.5, 24.5, 27.5, 30.5, 33.5)
D_AT = 45.5
COPY_LAG = 1.6
CHUNK_TIME = 5.8
MESH = pl.DeviceIdType.MESH


def runs(way, piece, hop, half):
    return 1 <= hop < half or (hop == half and piece // (PIECES // 2) == way)


def gathers(way, part, hop, half):
    return 1 <= hop < half or (hop == half and part // (PARTS // 2) == way)


def sources_of(slot, half):
    if slot == 0:
        return []
    if slot == 2 * half - 1:
        return [("gather", part, half, part // (PARTS // 2)) for part in range(PARTS)]
    hop, way = (slot + 1) // 2, (slot + 1) % 2
    return [("gather", part, hop, way) for part in range(PARTS)]


def schedule(half):
    ways, hops = (0, 1), range(1, half + 1)
    cost = dict(mul=0.45, sum=0.12, act=0.2, gather=0.05, down=0.9, back=0.35)
    rank = dict(gather=1, act=1, sum=1, mul=2, back=3, down=4)
    left = [("mul", piece, 0, 0) for piece in range(PIECES)]
    left += [
        ("sum", piece, hop, way)
        for piece in range(PIECES)
        for hop in hops
        for way in ways
        if runs(way, piece, hop, half)
    ]
    left += [("act", piece, 0, 0) for piece in range(PIECES)]
    left += [
        ("gather", part, hop, way)
        for part in range(PARTS)
        for hop in hops
        for way in ways
        if gathers(way, part, hop, half)
    ]
    left += [(kind, slot, 0, 0) for kind in ("down", "back") for slot in range(2 * half)]
    done, landing = {}, {}

    def ready(task):
        kind, index, hop, way = task
        per = PIECES // PARTS
        if kind == "mul":
            return max(X_AT, W_AT[index])
        if kind == "sum":
            needs = [done.get(("mul", index, 0, 0))]
            if runs(way, index, hop + 1, half):
                needs.append(landing.get(("sum", index, hop + 1, way)))
        elif kind == "act":
            needs = [landing.get(("sum", index, 1, side)) for side in ways]
        elif kind == "gather" and hop == 1:
            needs = [done.get(("act", index * per + k, 0, 0)) for k in range(per)]
        elif kind == "gather":
            needs = [landing.get(("gather", index, hop - 1, way))]
        elif kind == "down" and index == 0:
            needs = [D_AT] + [done.get(("act", piece, 0, 0)) for piece in range(PIECES)]
        elif kind == "down":
            needs = [D_AT] + [landing.get(source) for source in sources_of(index, half)]
        else:
            needs = [landing.get(("down", index, 0, 0))]
        return None if None in needs else max(needs)

    now, links, order = 0.0, {0: 0.0, 1: 0.0, "mate": D_AT}, []
    while left:
        waiting = [(ready(task), task) for task in left]
        waiting = [entry for entry in waiting if entry[0] is not None]
        now = max(now, min(entry[0] for entry in waiting))
        able = [entry for entry in waiting if entry[0] <= now]
        _, task = min(able, key=lambda entry: (rank[entry[1][0]], entry[0], entry[1]))
        left.remove(task)
        order.append(task)
        kind, _, _, way = task
        now += cost[kind]
        done[task] = now
        if kind in ("sum", "gather", "down"):
            link = "mate" if kind == "down" else way
            load = {
                "sum": CHUNK_TIME / PIECES,
                "gather": CHUNK_TIME / 2 / PARTS,
                "down": CHUNK_TIME / 8,
            }
            links[link] = max(links[link], now) + load[kind]
            landing[task] = links[link] + COPY_LAG
    return order


def expert_kernel(
    ring,
    idr_ref,
    gv_ref,
    tok_ref,
    wg_any,
    wu_any,
    wd_any,
    sg_ref,
    su_ref,
    sd_ref,
    out_ref,
    wg_ref,
    wu_ref,
    wd_ref,
    packed,
    mixing,
    x_near,
    x_far,
    x_all,
    w_send,
    w_all,
    d_send,
    d_own,
    d_far,
    parts,
    sum_out,
    sum_in,
    hidden,
    y_own,
    y_out,
    y_in,
    y_back,
    landed,
    route_sems,
    mate_sems,
    near_sems,
    far_sems,
    w_sems,
    sum_sems,
    gather_sems,
    y_sems,
    back_sems,
    load_sems,
):
    half = ring // 2
    local_tokens, width = tok_ref.shape
    rows = x_all.shape[0]
    chunk = rows // ring
    units = wg_ref.shape[1] // 2
    cols = units // PIECES
    slots = EXPERTS * CAP
    place = lax.axis_index("fsdp")
    z = place // 2
    side = place % 2
    seat = lax.axis_index("expert")
    high = seat // 16
    y = (seat // 2) % 8
    core = seat % 2
    expert = high * 4 + y // 2
    share = (y % 2) * 2 + core
    mate = {"fsdp": z * 2 + (1 - side)}
    sibling = {"expert": seat + 1 - 2 * core}
    step = {
        0: {"fsdp": ((z + 1) % ring) * 2 + side},
        1: {"fsdp": ((z + ring - 1) % ring) * 2 + side},
    }
    sends = []

    def remote(src, dst, sems, index, target):
        return pltpu.make_async_remote_copy(
            src_ref=src,
            dst_ref=dst,
            send_sem=sems.at[(0,) + index],
            recv_sem=sems.at[(1,) + index],
            device_id=target,
            device_id_type=MESH,
        )

    def send(*args):
        copy = remote(*args)
        copy.start()
        sends.append(copy)

    loads = [
        pltpu.make_async_copy(src, dst, load_sems.at[index])
        for index, (src, dst) in enumerate(((wg_any, wg_ref), (wu_any, wu_ref), (wd_any, wd_ref)))
    ]
    for load in loads:
        load.start()
    barrier = pltpu.get_barrier_semaphore()
    for target in (mate, step[0], step[1]):
        pl.semaphore_signal(barrier, inc=1, device_id=target, device_id_type=MESH)
    for other in range(1, 32):
        target = {"expert": (seat + other) % 32}
        pl.semaphore_signal(barrier, inc=1, device_id=target, device_id_type=MESH)

    def scaled(w_ref, s_ref, block, start):
        tiles = []
        for lane in range(cols // BLOCK):
            low = pl.multiple_of(start + lane * BLOCK, BLOCK)
            values = w_ref[block * BLOCK : (block + 1) * BLOCK, pl.ds(low, BLOCK)]
            scale = s_ref[block, start // BLOCK + lane]
            tiles.append((values.astype(jnp.float32) * scale).astype(jnp.bfloat16))
        return tiles

    def fill(dst, piece, owner):
        for block in range(width // BLOCK):
            low = block * BLOCK
            start = owner * units + piece * cols
            for index, (w_ref, s_ref) in enumerate(((wg_ref, sg_ref), (wu_ref, su_ref))):
                for lane, tile in enumerate(scaled(w_ref, s_ref, block, start)):
                    left = index * cols + lane * BLOCK
                    dst[piece, low : low + BLOCK, left : left + BLOCK] = tile

    def fill_down(dst, owner):
        for block in range(units // BLOCK):
            start = pl.multiple_of(owner * units + block * BLOCK, BLOCK)
            for lane in range(width // BLOCK):
                left = lane * BLOCK
                scale = sd_ref[lane, owner * (units // BLOCK) + block]
                values = wd_ref[pl.ds(start, BLOCK), left : left + BLOCK].astype(jnp.float32)
                dst[block * BLOCK : (block + 1) * BLOCK, left : left + BLOCK] = (
                    values * scale
                ).astype(jnp.bfloat16)

    def iota(shape, axis):
        return lax.broadcasted_iota(jnp.int32, shape, axis)

    def mask(test, kind):
        return jnp.where(test, 1.0, 0.0).astype(kind)

    square = (local_tokens, local_tokens)
    names = iota((EXPERTS, local_tokens), 0)
    picks = [mask(names == idr_ref[k : k + 1, :], jnp.float32) for k in range(2)]
    before = jnp.dot(
        (picks[0] + picks[1]).astype(jnp.bfloat16),
        mask(iota(square, 0) < iota(square, 1), jnp.bfloat16),
        preferred_element_type=jnp.float32,
    )
    spots = iota((slots, local_tokens), 0)
    chosen = jnp.zeros((slots, local_tokens), jnp.float32)
    shares = jnp.zeros((slots, local_tokens), jnp.float32)
    for k in range(2):
        rank = jnp.sum(before * picks[k], axis=0, keepdims=True).astype(jnp.int32)
        found = spots == idr_ref[k : k + 1, :] * CAP + rank
        chosen = chosen + mask(found, jnp.float32)
        shares = shares + jnp.where(found, gv_ref[k : k + 1, :], 0.0)
    mixing[...] = shares
    picked = jnp.dot(
        chosen.astype(jnp.bfloat16), tok_ref[...], preferred_element_type=jnp.float32
    )
    packed[...] = picked.reshape(packed.shape).astype(jnp.bfloat16)

    loads[0].wait()
    loads[1].wait()
    for piece in range(FIRST):
        fill(w_send, piece, 1 - side)
    pl.semaphore_wait(barrier, 34)
    my_block = core * 2 + high

    def block_of(turn):
        return core * 2 + (high + turn) % 2

    def send_piece(piece):
        send(w_send.at[piece], w_all.at[piece, width:, :], w_sems, (piece,), mate)

    def wait_bytes(ref, sem):
        pltpu.make_async_copy(ref, ref, sem).wait()

    for turn in range(2):
        for other in (4, 3, 5, 2, 6, 1, 7, 0):
            to_high = (high + turn) % 2
            to_y = (y + other) % 8
            src = packed.at[to_high * 4 + to_y // 2]
            dst = x_near.at[my_block, :, y]
            if turn == 0 and other == 0:
                pltpu.make_async_copy(src, dst, route_sems.at[1, 0]).start()
            else:
                target = {"expert": to_high * 16 + to_y * 2 + core}
                remote(src, dst, route_sems, (turn,), target).start()
    for piece in range(FIRST):
        send_piece(piece)
    for piece in range(FIRST, PIECES):
        fill(w_send, piece, 1 - side)
    for piece in range(PIECES):
        fill(w_all, piece, side)
    for turn in range(2):
        block = block_of(turn)
        wait_bytes(x_near.at[block], route_sems.at[1, turn])
        send(x_near.at[block], x_far.at[block], mate_sems, (turn,), mate)
        send(x_near.at[block], x_near.at[block], near_sems, (turn,), sibling)
    for piece in range(FIRST, PIECES):
        send_piece(piece)
    loads[2].wait()
    fill_down(d_send, 1 - side)
    send(d_send, d_far, w_sems, (PIECES,), mate)
    for turn in range(2):
        block = block_of(turn)
        remote(x_near.at[block], x_far.at[block], mate_sems, (turn,), mate).wait_recv()
        send(x_far.at[block], x_far.at[block], far_sems, (turn,), sibling)
    fill_down(d_own, side)
    for turn in range(2):
        block = (1 - core) * 2 + (high + turn) % 2
        remote(x_near.at[block], x_near.at[block], near_sems, (turn,), sibling).wait_recv()
        remote(x_far.at[block], x_far.at[block], far_sems, (turn,), sibling).wait_recv()
    part_rows = rows // 4
    for block in range(4):
        for index, source in enumerate((x_near, x_far)):
            values = source[block].astype(jnp.float32).reshape(part_rows, width)
            x_all[
                block * part_rows : (block + 1) * part_rows, index * width : (index + 1) * width
            ] = values.astype(jnp.bfloat16)

    def rows_of(index):
        return pl.ds(pl.multiple_of(index * chunk, chunk), chunk)

    def wait_sum(way, hop, piece):
        remote(
            sum_out.at[way, hop - 1, piece],
            sum_in.at[way, hop - 1, piece],
            sum_sems,
            (way, hop - 1, piece),
            step[way],
        ).wait_recv()

    def wait_hidden(way, hop, part):
        origin = (z + ring - hop) % ring if way == 0 else (z + hop) % ring
        remote(
            hidden.at[origin, part],
            hidden.at[origin, part],
            gather_sems,
            (way, hop - 1, part),
            step[way],
        ).wait_recv()

    arrived = set()

    def ready(way, hop, part):
        if (way, hop, part) not in arrived:
            arrived.add((way, hop, part))
            wait_hidden(way, hop, part)

    def origin_of(slot):
        if slot % 2 == 1:
            return (z + ring - (slot + 1) // 2) % ring
        return (z + slot // 2) % ring

    row_tile = rows // 3
    part_units = units // PARTS
    per_part = PIECES // PARTS
    for kind, index, hop, way in schedule(half):
        if kind == "mul":
            remote(
                w_send.at[index], w_all.at[index, width:, :], w_sems, (index,), mate
            ).wait_recv()
            for tile in range(3):
                low = tile * row_tile
                parts[index, low : low + row_tile, :] = jnp.dot(
                    x_all[low : low + row_tile, :],
                    w_all[index],
                    preferred_element_type=jnp.float32,
                )
        elif kind == "sum":
            owner = (z + hop) % ring if way == 0 else (z + ring - hop) % ring
            total = parts[index, rows_of(owner), :]
            if runs(way, index, hop + 1, half):
                wait_sum(way, hop + 1, index)
                total = total + sum_in[way, hop, index].astype(jnp.float32)
            sum_out[way, hop - 1, index] = total.astype(jnp.bfloat16)
            send(
                sum_out.at[way, hop - 1, index],
                sum_in.at[way, hop - 1, index],
                sum_sems,
                (way, hop - 1, index),
                step[way],
            )
        elif kind == "act":
            total = parts[index, rows_of(z), :]
            for side_way in range(2):
                wait_sum(side_way, 1, index)
                total = total + sum_in[side_way, 0, index].astype(jnp.float32)
            gate = total[:, :cols]
            act = gate / (1.0 + jnp.exp(-gate)) * total[:, cols:]
            low = (index % per_part) * cols
            hidden[z, index // per_part, :, low : low + cols] = act.astype(jnp.bfloat16)
        elif kind == "gather":
            if hop > 1:
                ready(way, hop - 1, index)
            origin = (z + ring - hop + 1) % ring if way == 0 else (z + hop - 1) % ring
            send(
                hidden.at[origin, index],
                hidden.at[origin, index],
                gather_sems,
                (way, hop - 1, index),
                step[way],
            )
        elif kind == "down":
            if index == 0:
                remote(d_send, d_far, w_sems, (PIECES,), mate).wait_recv()
            for _, part, source_hop, source_way in sources_of(index, half):
                ready(source_way, source_hop, part)
            origin = origin_of(index)
            own = jnp.zeros((chunk, width), jnp.float32)
            far = jnp.zeros((chunk, width), jnp.float32)
            for part in range(PARTS):
                low = part * part_units
                lhs = hidden[origin, part]
                far = far + jnp.dot(
                    lhs, d_far[low : low + part_units, :], preferred_element_type=jnp.float32
                )
                own = own + jnp.dot(
                    lhs, d_own[low : low + part_units, :], preferred_element_type=jnp.float32
                )
            y_own[index] = own
            y_out[index] = far.astype(jnp.bfloat16)
            send(y_out.at[index], y_in.at[index], y_sems, (index,), mate)
        else:
            remote(y_out.at[index], y_in.at[index], y_sems, (index,), mate).wait_recv()
            total = y_own[index] + y_in[index].astype(jnp.float32)
            y_back[index * 8 : index * 8 + 8] = total.reshape(8, 8, width).astype(jnp.bfloat16)
            origin = origin_of(index)
            block = origin // 3
            dst = landed.at[share, expert, origin % 3]
            for other in range(8):
                to_y = (y + other) % 8
                src = y_back.at[index * 8 + to_y]
                target = {"expert": (block % 2) * 16 + to_y * 2 + block // 2}
                copy = remote(src, dst, back_sems, (), target)
                if other > 0:
                    copy.start()
                else:
                    pl.when(block != my_block)(copy.start)
                    pl.when(block == my_block)(
                        pltpu.make_async_copy(src, dst, back_sems.at[1]).start
                    )

    wait_bytes(landed, back_sems.at[1])
    sums = landed[0].astype(jnp.float32)
    for index in range(1, 4):
        sums = sums + landed[index].astype(jnp.float32)
    out_ref[...] = lax.dot_general(
        mixing[...],
        sums.reshape(slots, width),
        (((0,), (0,)), ((), ())),
        precision=lax.Precision.HIGHEST,
        preferred_element_type=jnp.float32,
    )

    wait_bytes(packed.at[:7], route_sems.at[0, 0])
    wait_bytes(packed, route_sems.at[0, 1])
    wait_bytes(y_back.at[:93], back_sems.at[0])
    for copy in sends:
        copy.wait_send()


def shards(tokens, expert_ids, gate_values, w_gate, w_up, w_down, scale_gate, scale_up, scale_down):
    ring = lax.axis_size("fsdp") // 2
    local_tokens, width = tokens.shape
    rows = lax.axis_size("expert") * CAP
    units = w_gate.shape[1] // 2
    cols = units // PIECES
    half = ring // 2
    chunk = rows // ring
    vmem = pl.BlockSpec(memory_space=pltpu.VMEM)
    smem = pl.BlockSpec(memory_space=pltpu.SMEM)
    bf16, f32 = jnp.bfloat16, jnp.float32
    dma = pltpu.SemaphoreType.DMA
    anywhere = pl.BlockSpec(memory_space=pl.ANY)
    mixed = pl.pallas_call(
        functools.partial(expert_kernel, ring),
        out_shape=jax.ShapeDtypeStruct((local_tokens, width), f32),
        in_specs=[vmem] * 3 + [anywhere] * 3 + [smem] * 3,
        out_specs=vmem,
        scratch_shapes=[
            pltpu.VMEM(w_gate.shape, bf16),
            pltpu.VMEM(w_up.shape, bf16),
            pltpu.VMEM(w_down.shape, bf16),
            pltpu.VMEM((EXPERTS, 3, 8, width), bf16),
            pltpu.VMEM((EXPERTS * CAP, local_tokens), f32),
            pltpu.VMEM((4, 3, 8, 8, width), bf16),
            pltpu.VMEM((4, 3, 8, 8, width), bf16),
            pltpu.VMEM((rows, 2 * width), bf16),
            pltpu.VMEM((PIECES, width, 2 * cols), bf16),
            pltpu.VMEM((PIECES, 2 * width, 2 * cols), bf16),
            pltpu.VMEM((units, width), bf16),
            pltpu.VMEM((units, width), bf16),
            pltpu.VMEM((units, width), bf16),
            pltpu.VMEM((PIECES, rows, 2 * cols), f32),
            pltpu.VMEM((2, half, PIECES, chunk, 2 * cols), bf16),
            pltpu.VMEM((2, half, PIECES, chunk, 2 * cols), bf16),
            pltpu.VMEM((ring, PARTS, chunk, units // PARTS), bf16),
            pltpu.VMEM((ring, chunk, width), f32),
            pltpu.VMEM((ring, chunk, width), bf16),
            pltpu.VMEM((ring, chunk, width), bf16),
            pltpu.VMEM((ring * 8, 8, width), bf16),
            pltpu.VMEM((4, EXPERTS, 3, 8, width), bf16),
            dma((2, 2)),
            dma((2, 2)),
            dma((2, 2)),
            dma((2, 2)),
            dma((2, PIECES + 1)),
            dma((2, 2, half, PIECES)),
            dma((2, 2, half, PARTS)),
            dma((2, ring)),
            dma((2,)),
            dma((3,)),
        ],
        compiler_params=pltpu.CompilerParams(collective_id=0, has_side_effects=True),
        name="expert_layer",
    )(
        expert_ids.T,
        gate_values.T,
        tokens,
        w_gate,
        w_up,
        w_down,
        scale_gate,
        scale_up,
        scale_down.T,
    )
    return mixed.astype(bf16)


def solution(mesh):
    in_specs = (
        P("expert", "fsdp"),
        P("expert", None),
        P("expert", None),
        P("fsdp", "expert"),
        P("fsdp", "expert"),
        P("expert", "fsdp"),
        P("fsdp", "expert"),
        P("fsdp", "expert"),
        P("expert", "fsdp"),
    )
    out_specs = P("expert", "fsdp")
    return jax.shard_map(shards, mesh=mesh, in_specs=in_specs, out_specs=out_specs, check_vma=False)
```

time: 126 us -> 111 us (0.88)
  Pallas kernels: 122 us -> 109 us
  local copies, waits for them, and re-layouts: 4.16 us -> 0 us
  other arithmetic: 0 us -> 1.46 us
    pallas_call x1, Pallas kernels: 122 us -> 109 us  [shards(): pl.pallas_call(functools.partial(expert_kernel, ring), out_shape=jax.Shap...]
    unnamed x10 -> x0, local copies, waits for them, and re-layouts: 4.16 us -> none
    convert_element_type x0 -> x1, other arithmetic: none -> 1.46 us  [shards(): return mixed.astype(bf16)]
where the time goes in v3:
time: 111 us
  Pallas kernels  109 us (98%)
  other arithmetic  1.46 us (1%)
    pallas_call x1, Pallas kernels, shards(): pl.pallas_call(functools.partial(expert_kernel, ring), out_shape=jax.Shap...  109 us

profile of v3, /device:TPU:1, one launch (start us, length us, event | category | flops | bytes accessed | tf_op | source)
XLA Modules:
  0.0 110.7 jit_solution(4631168337817694543)
XLA Ops:
  0.0 109.2 %expert_layer.1 = f32[64,256]{1,0:T(8,128)} custom-call(s32[2,64]{1,0:T(2,128)} %bitcast.3, f32[2,64]{1,0:T(2,128)} %bitcast.4, bf16[64,256]{1,0:T(8,128)(2,1)} %tok_ref.1, bf16[256,2048]{1,0:T(8,128)(2,1)} %wg_any.1, bf16[256,2048]{1,0:T(8,128)(2,1)} %wu_any.1, bf16[2048,256]{1,0:T(8,128)(2,1)} %wd_any.1, f32[2,16]{1,0:T(2,128)} %sg_ref.1, f32[2,16]{1,0:T(2,128)} %su_ref.1, ...), custom_call_target="tpu_custom_call" | custom-call | tf_op jit(solution)/shard_map/expert_layer/pallas_call | solution.py:480
  109.2 1.5 %convert_element_type.3 = bf16[64,256]{1,0:T(8,128)(2,1)} convert(f32[64,256]{1,0:T(8,128)} %expert_layer.1) | non-fusion elementwise | flops 16384 | bytes 98304 | tf_op jit(solution)/shard_map/convert_element_type | solution.py:532

commit v4 on v3

--- a/solution.py
+++ b/solution.py
@@ -12,12 +12,12 @@
 CAP = 24
 PIECES = 8
 PARTS = 4
-FIRST = 2
-X_AT = 19.0
-W_AT = (8.0, 11.0, 18.5, 21.5, 24.5, 27.5, 30.5, 33.5)
-D_AT = 45.5
-COPY_LAG = 1.6
-CHUNK_TIME = 5.8
+FIRST = 3
+X_AT = 21.0
+W_AT = (7.5, 10.6, 13.7, 21.5, 24.6, 27.7, 30.8, 33.9)
+D_AT = 46.6
+COPY_LAG = 2.0
+CHUNK_TIME = 6.24
 MESH = pl.DeviceIdType.MESH
 
 
@@ -40,7 +40,7 @@
 
 def schedule(half):
     ways, hops = (0, 1), range(1, half + 1)
-    cost = dict(mul=0.45, sum=0.12, act=0.2, gather=0.05, down=0.9, back=0.35)
+    cost = dict(mul=0.45, sum=0.12, act=0.2, gather=0.05, down=0.28, back=0.35)
     rank = dict(gather=1, act=1, sum=1, mul=2, back=3, down=4)
     left = [("mul", piece, 0, 0) for piece in range(PIECES)]
     left += [
@@ -58,8 +58,9 @@
         for way in ways
         if gathers(way, part, hop, half)
     ]
-    left += [(kind, slot, 0, 0) for kind in ("down", "back") for slot in range(2 * half)]
-    done, landing = {}, {}
+    left += [("down", slot, part, 0) for slot in range(2 * half) for part in range(PARTS)]
+    left += [("back", slot, 0, 0) for slot in range(2 * half)]
+    done, landing, joined = {}, {}, {}
 
     def ready(task):
         kind, index, hop, way = task
@@ -77,11 +78,11 @@
         elif kind == "gather":
             needs = [landing.get(("gather", index, hop - 1, way))]
         elif kind == "down" and index == 0:
-            needs = [D_AT] + [done.get(("act", piece, 0, 0)) for piece in range(PIECES)]
+            needs = [D_AT] + [done.get(("act", hop * per + k, 0, 0)) for k in range(per)]
         elif kind == "down":
-            needs = [D_AT] + [landing.get(source) for source in sources_of(index, half)]
+            needs = [D_AT, landing.get(sources_of(index, half)[hop])]
         else:
-            needs = [landing.get(("down", index, 0, 0))]
+            needs = [landing.get(("down", index))]
         return None if None in needs else max(needs)
 
     now, links, order = 0.0, {0: 0.0, 1: 0.0, "mate": D_AT}, []
@@ -96,15 +97,16 @@
         kind, _, _, way = task
         now += cost[kind]
         done[task] = now
-        if kind in ("sum", "gather", "down"):
-            link = "mate" if kind == "down" else way
-            load = {
-                "sum": CHUNK_TIME / PIECES,
-                "gather": CHUNK_TIME / 2 / PARTS,
-                "down": CHUNK_TIME / 8,
-            }
-            links[link] = max(links[link], now) + load[kind]
-            landing[task] = links[link] + COPY_LAG
+        if kind == "sum" or kind == "gather":
+            load = CHUNK_TIME / PIECES if kind == "sum" else CHUNK_TIME / 2 / PARTS
+            links[way] = max(links[way], now) + load
+            landing[task] = links[way] + COPY_LAG
+        elif kind == "down":
+            slot = task[1]
+            joined[slot] = joined.get(slot, 0) + 1
+            if joined[slot] == PARTS:
+                links["mate"] = max(links["mate"], now) + CHUNK_TIME / 8
+                landing[("down", slot)] = links["mate"] + COPY_LAG
     return order
 
 
@@ -138,6 +140,7 @@
     sum_in,
     hidden,
     y_own,
+    y_far,
     y_out,
     y_in,
     y_back,
@@ -152,6 +155,7 @@
     y_sems,
     back_sems,
     load_sems,
+    spread,
 ):
     half = ring // 2
     local_tokens, width = tok_ref.shape
@@ -199,11 +203,17 @@
     for load in loads:
         load.start()
     barrier = pltpu.get_barrier_semaphore()
-    for target in (mate, step[0], step[1]):
-        pl.semaphore_signal(barrier, inc=1, device_id=target, device_id_type=MESH)
-    for other in range(1, 32):
-        target = {"expert": (seat + other) % 32}
-        pl.semaphore_signal(barrier, inc=1, device_id=target, device_id_type=MESH)
+
+    def along(count):
+        return {"expert": high * 16 + (y + 8 + count) % 8 * 2 + core}
+
+    across = {"expert": (seat + 16) % 32}
+
+    def tell(sem, targets):
+        for target in targets:
+            pl.semaphore_signal(sem, inc=1, device_id=target, device_id_type=MESH)
+
+    tell(barrier, (mate, step[0], step[1], sibling, along(1), along(-1), across))
 
     def scaled(w_ref, s_ref, block, start):
         tiles = []
@@ -240,6 +250,25 @@
     def mask(test, kind):
         return jnp.where(test, 1.0, 0.0).astype(kind)
 
+    loads[0].wait()
+    loads[1].wait()
+    for piece in range(FIRST):
+        fill(w_send, piece, 1 - side)
+    pl.semaphore_wait(barrier, 7)
+    my_block = core * 2 + high
+
+    def block_of(turn):
+        return core * 2 + (high + turn) % 2
+
+    def send_piece(piece):
+        send(w_send.at[piece], w_all.at[piece, width:, :], w_sems, (piece,), mate)
+
+    def wait_bytes(ref, sem):
+        pltpu.make_async_copy(ref, ref, sem).wait()
+
+    for piece in range(FIRST):
+        send_piece(piece)
+    tell(spread.at[0], (along(1), along(-1)))
     square = (local_tokens, local_tokens)
     names = iota((EXPERTS, local_tokens), 0)
     picks = [mask(names == idr_ref[k : k + 1, :], jnp.float32) for k in range(2)]
@@ -262,22 +291,14 @@
     )
     packed[...] = picked.reshape(packed.shape).astype(jnp.bfloat16)
 
-    loads[0].wait()
-    loads[1].wait()
-    for piece in range(FIRST):
-        fill(w_send, piece, 1 - side)
-    pl.semaphore_wait(barrier, 34)
-    my_block = core * 2 + high
-
-    def block_of(turn):
-        return core * 2 + (high + turn) % 2
-
-    def send_piece(piece):
-        send(w_send.at[piece], w_all.at[piece, width:, :], w_sems, (piece,), mate)
-
-    def wait_bytes(ref, sem):
-        pltpu.make_async_copy(ref, ref, sem).wait()
-
+    pl.semaphore_wait(spread.at[0], 2)
+    tell(spread.at[1], (along(2), along(-2)))
+    fill(w_send, FIRST, 1 - side)
+    pl.semaphore_wait(spread.at[1], 2)
+    tell(spread.at[2], (across,))
+    fill(w_send, FIRST + 1, 1 - side)
+    pl.semaphore_wait(spread.at[2], 1)
+    tell(spread.at[3], (sibling,))
     for turn in range(2):
         for other in (4, 3, 5, 2, 6, 1, 7, 0):
             to_high = (high + turn) % 2
@@ -289,9 +310,7 @@
             else:
                 target = {"expert": to_high * 16 + to_y * 2 + core}
                 remote(src, dst, route_sems, (turn,), target).start()
-    for piece in range(FIRST):
-        send_piece(piece)
-    for piece in range(FIRST, PIECES):
+    for piece in range(FIRST + 2, PIECES):
         fill(w_send, piece, 1 - side)
     for piece in range(PIECES):
         fill(w_all, piece, side)
@@ -359,6 +378,8 @@
     row_tile = rows // 3
     part_units = units // PARTS
     per_part = PIECES // PARTS
+    joined = {}
+    told = False
     for kind, index, hop, way in schedule(half):
         if kind == "mul":
             remote(
@@ -406,33 +427,40 @@
                 step[way],
             )
         elif kind == "down":
-            if index == 0:
+            if not joined:
                 remote(d_send, d_far, w_sems, (PIECES,), mate).wait_recv()
-            for _, part, source_hop, source_way in sources_of(index, half):
-                ready(source_way, source_hop, part)
-            origin = origin_of(index)
-            own = jnp.zeros((chunk, width), jnp.float32)
-            far = jnp.zeros((chunk, width), jnp.float32)
-            for part in range(PARTS):
-                low = part * part_units
-                lhs = hidden[origin, part]
-                far = far + jnp.dot(
-                    lhs, d_far[low : low + part_units, :], preferred_element_type=jnp.float32
-                )
-                own = own + jnp.dot(
-                    lhs, d_own[low : low + part_units, :], preferred_element_type=jnp.float32
-                )
+            if index > 0:
+                _, _, source_hop, source_way = sources_of(index, half)[hop]
+                ready(source_way, source_hop, hop)
+            lhs = hidden[origin_of(index), hop]
+            low = hop * part_units
+            far = jnp.dot(
+                lhs, d_far[low : low + part_units, :], preferred_element_type=jnp.float32
+            )
+            own = jnp.dot(
+                lhs, d_own[low : low + part_units, :], preferred_element_type=jnp.float32
+            )
+            count = joined[index] = joined.get(index, 0) + 1
+            if count > 1:
+                far = far + y_far[index]
+                own = own + y_own[index]
             y_own[index] = own
-            y_out[index] = far.astype(jnp.bfloat16)
-            send(y_out.at[index], y_in.at[index], y_sems, (index,), mate)
+            if count < PARTS:
+                y_far[index] = far
+            else:
+                y_out[index] = far.astype(jnp.bfloat16)
+                send(y_out.at[index], y_in.at[index], y_sems, (index,), mate)
         else:
+            if not told:
+                pl.semaphore_wait(spread.at[3], 1)
+                told = True
             remote(y_out.at[index], y_in.at[index], y_sems, (index,), mate).wait_recv()
             total = y_own[index] + y_in[index].astype(jnp.float32)
             y_back[index * 8 : index * 8 + 8] = total.reshape(8, 8, width).astype(jnp.bfloat16)
             origin = origin_of(index)
             block = origin // 3
             dst = landed.at[share, expert, origin % 3]
-            for other in range(8):
+            for other in (4, 3, 5, 2, 6, 1, 7, 0):
                 to_y = (y + other) % 8
                 src = y_back.at[index * 8 + to_y]
                 target = {"expert": (block % 2) * 16 + to_y * 2 + block // 2}
@@ -501,6 +529,7 @@
             pltpu.VMEM((2, half, PIECES, chunk, 2 * cols), bf16),
             pltpu.VMEM((ring, PARTS, chunk, units // PARTS), bf16),
             pltpu.VMEM((ring, chunk, width), f32),
+            pltpu.VMEM((ring, chunk, width), f32),
             pltpu.VMEM((ring, chunk, width), bf16),
             pltpu.VMEM((ring, chunk, width), bf16),
             pltpu.VMEM((ring * 8, 8, width), bf16),
@@ -515,6 +544,7 @@
             dma((2, ring)),
             dma((2,)),
             dma((3,)),
+            pltpu.SemaphoreType.REGULAR((4,)),
         ],
         compiler_params=pltpu.CompilerParams(collective_id=0, has_side_effects=True),
         name="expert_layer",

time: 111 us -> 111 us (level)
  no operation moved by 1% of the time
where the time goes in v4:
time: 111 us
  Pallas kernels  110 us (99%)
  other arithmetic  1.46 us (1%)
    pallas_call x1, Pallas kernels, shards(): pl.pallas_call(functools.partial(expert_kernel, ring), out_shape=jax.Shap...  110 us

profile of v4, /device:TPU:1, one launch (start us, length us, event | category | flops | bytes accessed | tf_op | source)
XLA Modules:
  0.0 111.0 jit_solution(10197356484138321018)
XLA Ops:
  0.0 109.6 %expert_layer.1 = f32[64,256]{1,0:T(8,128)} custom-call(s32[2,64]{1,0:T(2,128)} %bitcast.3, f32[2,64]{1,0:T(2,128)} %bitcast.4, bf16[64,256]{1,0:T(8,128)(2,1)} %tok_ref.1, bf16[256,2048]{1,0:T(8,128)(2,1)} %wg_any.1, bf16[256,2048]{1,0:T(8,128)(2,1)} %wu_any.1, bf16[2048,256]{1,0:T(8,128)(2,1)} %wd_any.1, f32[2,16]{1,0:T(2,128)} %sg_ref.1, f32[2,16]{1,0:T(2,128)} %su_ref.1, ...), custom_call_target="tpu_custom_call" | custom-call | tf_op jit(solution)/shard_map/expert_layer/pallas_call | solution.py:508
  109.6 1.5 %convert_element_type.3 = bf16[64,256]{1,0:T(8,128)(2,1)} convert(f32[64,256]{1,0:T(8,128)} %expert_layer.1) | non-fusion elementwise | flops 16384 | bytes 98304 | tf_op jit(solution)/shard_map/convert_element_type | solution.py:562

commit v5 on v4

--- a/solution.py
+++ b/solution.py
@@ -50,6 +50,7 @@
         for way in ways
         if runs(way, piece, hop, half)
     ]
+    sums = left[PIECES:]
     left += [("act", piece, 0, 0) for piece in range(PIECES)]
     left += [
         ("gather", part, hop, way)
@@ -75,6 +76,7 @@
             needs = [landing.get(("sum", index, 1, side)) for side in ways]
         elif kind == "gather" and hop == 1:
             needs = [done.get(("act", index * per + k, 0, 0)) for k in range(per)]
+            needs += [done.get(other) for other in sums]
         elif kind == "gather":
             needs = [landing.get(("gather", index, hop - 1, way))]
         elif kind == "down" and index == 0:
@@ -250,25 +252,6 @@
     def mask(test, kind):
         return jnp.where(test, 1.0, 0.0).astype(kind)
 
-    loads[0].wait()
-    loads[1].wait()
-    for piece in range(FIRST):
-        fill(w_send, piece, 1 - side)
-    pl.semaphore_wait(barrier, 7)
-    my_block = core * 2 + high
-
-    def block_of(turn):
-        return core * 2 + (high + turn) % 2
-
-    def send_piece(piece):
-        send(w_send.at[piece], w_all.at[piece, width:, :], w_sems, (piece,), mate)
-
-    def wait_bytes(ref, sem):
-        pltpu.make_async_copy(ref, ref, sem).wait()
-
-    for piece in range(FIRST):
-        send_piece(piece)
-    tell(spread.at[0], (along(1), along(-1)))
     square = (local_tokens, local_tokens)
     names = iota((EXPERTS, local_tokens), 0)
     picks = [mask(names == idr_ref[k : k + 1, :], jnp.float32) for k in range(2)]
@@ -291,14 +274,32 @@
     )
     packed[...] = picked.reshape(packed.shape).astype(jnp.bfloat16)
 
+    loads[0].wait()
+    loads[1].wait()
+    fill(w_send, 0, 1 - side)
+    pl.semaphore_wait(barrier, 7)
+    my_block = core * 2 + high
+
+    def block_of(turn):
+        return core * 2 + (high + turn) % 2
+
+    def send_piece(piece):
+        send(w_send.at[piece], w_all.at[piece, width:, :], w_sems, (piece,), mate)
+
+    def wait_bytes(ref, sem):
+        pltpu.make_async_copy(ref, ref, sem).wait()
+
+    tell(spread.at[0], (along(1), along(-1)))
+    send_piece(0)
+    fill(w_send, 1, 1 - side)
+    send_piece(1)
     pl.semaphore_wait(spread.at[0], 2)
     tell(spread.at[1], (along(2), along(-2)))
-    fill(w_send, FIRST, 1 - side)
+    fill(w_send, 2, 1 - side)
+    send_piece(2)
     pl.semaphore_wait(spread.at[1], 2)
     tell(spread.at[2], (across,))
-    fill(w_send, FIRST + 1, 1 - side)
     pl.semaphore_wait(spread.at[2], 1)
-    tell(spread.at[3], (sibling,))
     for turn in range(2):
         for other in (4, 3, 5, 2, 6, 1, 7, 0):
             to_high = (high + turn) % 2
@@ -310,7 +311,8 @@
             else:
                 target = {"expert": to_high * 16 + to_y * 2 + core}
                 remote(src, dst, route_sems, (turn,), target).start()
-    for piece in range(FIRST + 2, PIECES):
+    tell(spread.at[3], (sibling,))
+    for piece in range(FIRST, PIECES):
         fill(w_send, piece, 1 - side)
     for piece in range(PIECES):
         fill(w_all, piece, side)
@@ -324,23 +326,27 @@
     loads[2].wait()
     fill_down(d_send, 1 - side)
     send(d_send, d_far, w_sems, (PIECES,), mate)
+    part_rows = rows // 4
+
+    def assemble(source, index, block):
+        values = source[block].astype(jnp.float32).reshape(part_rows, width)
+        span = pl.ds(pl.multiple_of(block * part_rows, part_rows), part_rows)
+        x_all[span, index * width : (index + 1) * width] = values.astype(jnp.bfloat16)
+
+    for turn in range(2):
+        assemble(x_near, 0, block_of(turn))
     for turn in range(2):
         block = block_of(turn)
         remote(x_near.at[block], x_far.at[block], mate_sems, (turn,), mate).wait_recv()
         send(x_far.at[block], x_far.at[block], far_sems, (turn,), sibling)
-    fill_down(d_own, side)
+    for turn in range(2):
+        assemble(x_far, 1, block_of(turn))
     for turn in range(2):
         block = (1 - core) * 2 + (high + turn) % 2
         remote(x_near.at[block], x_near.at[block], near_sems, (turn,), sibling).wait_recv()
+        assemble(x_near, 0, block)
         remote(x_far.at[block], x_far.at[block], far_sems, (turn,), sibling).wait_recv()
-    part_rows = rows // 4
-    for block in range(4):
-        for index, source in enumerate((x_near, x_far)):
-            values = source[block].astype(jnp.float32).reshape(part_rows, width)
-            x_all[
-                block * part_rows : (block + 1) * part_rows, index * width : (index + 1) * width
-            ] = values.astype(jnp.bfloat16)
-
+        assemble(x_far, 1, block)
     def rows_of(index):
         return pl.ds(pl.multiple_of(index * chunk, chunk), chunk)
 
@@ -428,6 +434,7 @@
             )
         elif kind == "down":
             if not joined:
+                fill_down(d_own, side)
                 remote(d_send, d_far, w_sems, (PIECES,), mate).wait_recv()
             if index > 0:
                 _, _, source_hop, source_way = sources_of(index, half)[hop]

time: 111 us -> 111 us (level)
  no operation moved by 1% of the time
where the time goes in v5:
time: 111 us
  Pallas kernels  109 us (98%)
  other arithmetic  1.46 us (1%)
    pallas_call x1, Pallas kernels, shards(): pl.pallas_call(functools.partial(expert_kernel, ring), out_shape=jax.Shap...  109 us

profile of v5, /device:TPU:1, one launch (start us, length us, event | category | flops | bytes accessed | tf_op | source)
XLA Modules:
  0.0 110.7 jit_solution(17570939471864515999)
XLA Ops:
  0.0 109.2 %expert_layer.1 = f32[64,256]{1,0:T(8,128)} custom-call(s32[2,64]{1,0:T(2,128)} %bitcast.3, f32[2,64]{1,0:T(2,128)} %bitcast.4, bf16[64,256]{1,0:T(8,128)(2,1)} %tok_ref.1, bf16[256,2048]{1,0:T(8,128)(2,1)} %wg_any.1, bf16[256,2048]{1,0:T(8,128)(2,1)} %wu_any.1, bf16[2048,256]{1,0:T(8,128)(2,1)} %wd_any.1, f32[2,16]{1,0:T(2,128)} %sg_ref.1, f32[2,16]{1,0:T(2,128)} %su_ref.1, ...), custom_call_target="tpu_custom_call" | custom-call | tf_op jit(solution)/shard_map/expert_layer/pallas_call | solution.py:515
  109.2 1.5 %convert_element_type.3 = bf16[64,256]{1,0:T(8,128)(2,1)} convert(f32[64,256]{1,0:T(8,128)} %expert_layer.1) | non-fusion elementwise | flops 16384 | bytes 98304 | tf_op jit(solution)/shard_map/convert_element_type | solution.py:569
